TPU v7x, 32 devices: a whole 2x2x4 slice. The times are simulated.
32 devices in a mesh: dp: 4 (over y, x), seq: 4 (over z), feat: 2 (over core).
Axes of the slice: x: 2, y: 2, z: 4, core: 2. Of those that a mesh axis runs over, the one named last changes fastest.
Arguments:
- tokens: bfloat16 [16384, 2048], P(('dp', 'seq')), parts along dimension 0, may hold values from -6 to 6
- w_query: bfloat16 [2048, 256], P(None, 'feat'), may hold values from -0.125 to 0.125
- w_key: bfloat16 [2048, 256], P(None, 'feat'), may hold values from -0.125 to 0.125
- value_weight: bfloat16 [2048, 2048], P(None, 'feat'), may hold values from -0.125 to 0.125
- w_out: bfloat16 [2048, 2048], P(None, 'feat'), may hold values from -0.125 to 0.125
Outputs:
- mixed: bfloat16 [16384, 2048], P(('dp', 'seq'), 'feat'), parts along dimension 0
There are 4 independent parts, one for each index of `dp`. A program takes and returns all parts, laid end to end along the dimension named above; an argument that names none is the same for every part. Nothing has to cross between parts.
All inputs are finite; a program needn't handle non-finite values.
Results may differ from a plain program's by a relative error of at most 0.009.
Values may be sent and summed in bfloat16 or wider, within the bound.
No kernel may reach another device: no remote copies, remote signals or barrier semaphores. Data moves between devices by JAX's collectives and lax.ppermute only.
A program may use at most 64 MiB of HBM per device.

v0:
```python
import jax
import jax.numpy as jnp
from jax import lax
from jax.sharding import PartitionSpec as P

DK = 16
DV = 128


def key_features(key_rows):
    as_float = key_rows.astype(jnp.float32)
    row_count = key_rows.shape[0]
    head_total = key_rows.shape[1]
    linear = jnp.transpose(as_float, (1, 2, 0))
    square = jnp.einsum("nha,nhb->habn", as_float, as_float).reshape(head_total, -1, row_count)
    ones_row = jnp.ones((head_total, 1, row_count), jnp.float32)
    return jnp.concatenate([ones_row, linear, square], axis=1).astype(jnp.bfloat16)


def query_features(query_rows):
    as_float = query_rows.astype(jnp.float32)
    row_count = query_rows.shape[0]
    head_total = query_rows.shape[1]
    linear = jnp.transpose(as_float, (1, 2, 0)) * 0.25
    square = jnp.einsum("nha,nhb->habn", as_float, as_float).reshape(head_total, -1, row_count) * (
        1.0 / 32.0
    )
    ones_row = jnp.ones((head_total, 1, row_count), jnp.float32)
    return jnp.concatenate([ones_row, linear, square], axis=1)


def local(tokens, w_query, w_key, value_weight, w_out):
    row_count = tokens.shape[0]
    local_heads = value_weight.shape[1] // DV
    query_rows = (
        jnp.dot(tokens, w_query, preferred_element_type=jnp.float32)
        .astype(jnp.bfloat16)
        .reshape(row_count, local_heads, DK)
    )
    key_rows = (
        jnp.dot(tokens, w_key, preferred_element_type=jnp.float32)
        .astype(jnp.bfloat16)
        .reshape(row_count, local_heads, DK)
    )
    value_matrix = (
        jnp.dot(tokens, value_weight, preferred_element_type=jnp.float32)
        .astype(jnp.bfloat16)
        .reshape(row_count, local_heads, DV)
    )
    block_state = jnp.einsum(
        "hfn,nhd->hfd", key_features(key_rows), value_matrix, preferred_element_type=jnp.float32
    )
    zero_state = jnp.zeros(block_state.shape, jnp.float32)
    my_block = lax.axis_index("seq")
    piece = lax.all_gather(
        block_state[None].astype(jnp.bfloat16), "seq", axis=0, tiled=True
    ).astype(jnp.float32)
    order = lax.broadcasted_iota(jnp.int32, (piece.shape[0],), 0)
    keep = (order < my_block).astype(jnp.float32)
    earlier = zero_state + jnp.sum(piece * keep[:, None, None, None], axis=0)
    scores = (
        jnp.einsum("nha,mha->hnm", query_rows, key_rows, preferred_element_type=jnp.float32) * 0.25
    )
    causal = lax.broadcasted_iota(jnp.int32, (row_count, row_count), 0) >= lax.broadcasted_iota(
        jnp.int32, (row_count, row_count), 1
    )
    weight_tensors = jnp.where(causal[None], 1.0 + scores + 0.5 * scores * scores, 0.0).astype(
        jnp.bfloat16
    )
    local_portion = jnp.einsum(
        "iot,tiw->oiw", weight_tensors, value_matrix, preferred_element_type=jnp.float32
    )
    carried = jnp.einsum(
        "hfn,hfd->nhd", query_features(query_rows), earlier, precision=lax.Precision.HIGHEST
    )
    numerator = carried + local_portion
    scale = lax.rsqrt(jnp.mean(numerator * numerator, axis=-1, keepdims=True) + 1e-06)
    normalized_rows = (numerator * scale).reshape(row_count, local_heads * DV).astype(jnp.bfloat16)
    mixed = jnp.dot(
        lax.all_gather(normalized_rows, "feat", axis=1, tiled=True),
        w_out,
        preferred_element_type=jnp.float32,
    )
    return mixed.astype(jnp.bfloat16)


def solution(mesh):
    placed = (
        P(("dp", "seq"), None),
        P(None, "feat"),
        P(None, "feat"),
        P(None, "feat"),
        P(None, "feat"),
    )
    return jax.shard_map(
        local, mesh=mesh, in_specs=placed, out_specs=P(("dp", "seq"), "feat"), check_vma=False
    )
```

profile of v0, /device:TPU:0, one launch (start us, length us, event | category | flops | bytes accessed | tf_op | source)
XLA Modules:
  0.0 135.8 jit_solution(15695235256979759861)
XLA Ops:
  6.5 0.0 copy-start
  6.5 0.0 all-gather.6.cloned.1.call-start
  6.5 1.0 copy-done
  7.6 0.0 copy-start.3
  7.6 3.9 %convolution_convert_fusion.3 = bf16[1024,128]{0,1:T(8,128)(2,1)S(1)} fusion(bf16[1024,2048]{1,0:T(8,128)(2,1)} %param.5, bf16[2048,128]{1,0:T(8,128)(2,1)S(1)} %copy-done), kind=kOutput, calls=%fused_computation.30 | convolution fusion | flops 537001984 | bytes 4980736 | tf_op jit(solution)/shard_map/dot_general | solution.py:41
  11.4 0.0 copy-start.1
  11.5 1.3 multiply_convert_fusion
  12.8 0.0 copy-done.3
  12.8 0.8 copy-done.1
  13.6 4.8 %convolution_convert_fusion.1 = bf16[1024,1024]{0,1:T(8,128)(2,1)S(1)} fusion(bf16[1024,2048]{1,0:T(8,128)(2,1)S(1)} %copy-done.1, bf16[2048,1024]{1,0:T(8,128)(2,1)S(1)} %copy-done.3), kind=kOutput, calls=%fused_computation.27 | convolution fusion | flops 4296015872 | bytes 10485760 | tf_op jit(solution)/shard_map/dot_general | solution.py:46
  18.5 0.0 copy-start.4
  18.5 0.0 copy-start.2
  18.5 1.7 %fusion.20 = bf16[8,273,128]{2,1,0:T(8,128)(2,1)S(1)} fusion(bf16[1024,8,128]{0,2,1:T(8,128)(2,1)S(1)} %bitcast.51, bf16[8,256,1024]{2,1,0:T(8,128)(2,1)S(1)} %bitcast.47, bf16[8,16,1024]{2,1,0:T(8,128)(2,1)S(1)} %bitcast.49, bf16[273]{0:T(512)(128)(2,1)S(1)} %pad.3.clone), kind=kOutput, calls=%fused_computation.28 | convolution fusion | flops 586220544 | bytes 7113250 | tf_op jit(solution)/shard_map/hfn,nhd->hfd/dot_general | solution.py:50
  20.2 0.0 copy-done.4
  20.2 0.9 copy.10
  21.1 0.0 all-gather.6.cloned.1.call-update
  21.1 0.0 all-gather.4.cloned.1.call-start
  21.2 0.3 iota_compare_fusion
  21.5 0.0 copy-done.2
  21.5 3.7 %convolution_convert_fusion.2 = bf16[1024,128]{0,1:T(8,128)(2,1)S(1)} fusion(bf16[1024,2048]{1,0:T(8,128)(2,1)} %param.5, bf16[2048,128]{1,0:T(8,128)(2,1)S(1)} %copy-done.2), kind=kOutput, calls=%fused_computation.29 | convolution fusion | flops 537001984 | bytes 4980736 | tf_op jit(solution)/shard_map/dot_general | solution.py:36
  25.3 4.4 %multiply_multiply_fusion = f32[8,1024,16,16]{1,2,3,0:T(8,128)} fusion(f32[8,1024,16]{1,2,0:T(8,128)S(1)} %convert_bitcast_fusion), kind=kLoop, calls=%fused_computation.8 | loop fusion | flops 4194304 | bytes 8912896 | tf_op jit(solution)/shard_map/mul | solution.py:25
  29.8 42.7 %all-gather.6.cloned.1.call-done = bf16[32,273,128]{2,0,1:T(8,128)(2,1)} async-done(((bf16[8,273,128]{2,0,1:T(8,128)(2,1)}), bf16[32,273,128]{2,0,1:T(8,128)(2,1)}) %all-gather.6.cloned.1.call-update) | async-done | bytes 2236432 | tf_op jit(solution)/shard_map/all_gather | solution.py:55
  72.5 2.8 %fusion.13 = f32[8,273,128]{2,0,1:T(8,128)S(1)} fusion(bf16[32,273,128]{2,0,1:T(8,128)(2,1)} %all-gather.6.cloned.1.call-done, f32[4]{0:T(128)S(1)} %compare_convert_fusion), kind=kLoop, calls=%fused_computation.17 | loop fusion | flops 3075072 | bytes 3354640 | tf_op jit(solution)/shard_map/reduce_sum | solution.py:60
  75.4 12.1 %fusion.2 = f32[8,128,1024]{2,1,0:T(8,128)} fusion(f32[8,256,1024]{2,1,0:T(8,128)} %bitcast.45, f32[8,16,1024]{2,1,0:T(8,128)S(1)} %fusion.24, f32[273]{0:T(512)S(1)} %pad.clone, f32[8,273,128]{2,0,1:T(8,128)S(1)} %fusion.13), kind=kOutput, calls=%fused_computation.3 | convolution fusion | flops 3439607808 | bytes 14226500 | tf_op jit(solution)/shard_map/hfn,hfd->nhd/dot_general | solution.py:73
  87.4 16.0 %fusion.14 = (f32[1024,8]{0,1:T(8,128)S(1)}, f32[8,128,1024]{2,1,0:T(8,128)}) fusion(f32[8,128,1024]{2,1,0:T(8,128)} %fusion.2, bf16[1024,8,128]{0,2,1:T(8,128)(2,1)} %bitcast.52, pred[1024,1024]{1,0:T(8,128)(4,1)S(1)} %iota_compare_fusion, bf16[1024,8,16]{0,2,1:T(8,128)(2,1)S(1)} %bitcast.48, bf16[1024,8,16]{0,2,1:T(8,128)(2,1)S(1)} %bitcast.50), kind=kOutput, calls=%fused_computation.20 | convolution fusion | flops 2477776896 | bytes 12091392 | tf_op jit(solution)/shard_map/iot,tiw->oiw/dot_general | solution.py:70
  103.4 4.1 %fusion.15 = bf16[1024,8,128]{0,2,1:T(8,128)(2,1)} fusion(f32[8,128,1024]{2,1,0:T(8,128)} %get-tuple-element.6, f32[1024,8]{0,1:T(8,128)S(1)} %add_rsqrt_fusion), kind=kLoop, calls=%fused_computation.21 | loop fusion | flops 2097152 | bytes 6324224 | tf_op jit(solution)/shard_map/convert_element_type | solution.py:78
  107.5 0.0 all-gather.4.cloned.1.call-update
  107.6 12.0 %all-gather.4.cloned.1.call-done = bf16[1024,2048]{0,1:T(8,128)(2,1)} async-done(((bf16[1024,1024]{0,1:T(8,128)(2,1)}), bf16[1024,2048]{0,1:T(8,128)(2,1)}) %all-gather.4.cloned.1.call-update) | async-done | bytes 4194320 | tf_op jit(solution)/shard_map/all_gather | solution.py:80
  119.6 9.4 %convolution_convert_fusion = bf16[1024,1024]{1,0:T(8,128)(2,1)} fusion(bf16[1024,2048]{0,1:T(8,128)(2,1)} %all-gather.4.cloned.1.call-done, bf16[2048,1024]{1,0:T(8,128)(2,1)} %param.9), kind=kOutput, calls=%fused_computation.26 | convolution fusion | flops 4296015872 | bytes 10485760 | tf_op jit(solution)/shard_map/dot_general | solution.py:79
  (7 shorter events, 0.2 us)
Async XLA Ops:
  6.5 1.0 copy-start
  6.5 66.0 %all-gather.6.cloned.1.call-start = ((), (), s32[]{:S(2)}) async-start(), calls=%async_computation.1 | async-start | bytes 2795520 | tf_op jit(solution)/shard_map/all_gather | solution.py:55
  7.6 5.2 %copy-start.3 = (bf16[2048,1024]{1,0:T(8,128)(2,1)S(1)}, bf16[2048,1024]{1,0:T(8,128)(2,1)}, u32[]{:S(2)}) copy-start(bf16[2048,1024]{1,0:T(8,128)(2,1)} %param.8) | copy-start | bytes 12582916
  11.4 2.2 %copy-start.1 = (bf16[1024,2048]{1,0:T(8,128)(2,1)S(1)}, bf16[1024,2048]{1,0:T(8,128)(2,1)}, u32[]{:S(2)}) copy-start(bf16[1024,2048]{1,0:T(8,128)(2,1)} %param.5) | copy-start | bytes 12582916
  18.5 1.7 %copy-start.4 = (bf16[1024,1024]{0,1:T(8,128)(2,1)}, bf16[1024,1024]{0,1:T(8,128)(2,1)S(1)}, u32[]{:S(2)}) copy-start(bf16[1024,1024]{0,1:T(8,128)(2,1)S(1)} %convolution_convert_fusion.1) | copy-start | bytes 6291460
  18.5 3.0 %copy-start.2 = (bf16[2048,128]{1,0:T(8,128)(2,1)S(1)}, bf16[2048,128]{1,0:T(8,128)(2,1)}, u32[]{:S(2)}) copy-start(bf16[2048,128]{1,0:T(8,128)(2,1)} %param.6) | copy-start | bytes 1572868
  21.1 98.4 %all-gather.4.cloned.1.call-start = ((), (), s32[]{:S(2)}) async-start(), calls=%async_computation | async-start | bytes 6291456 | tf_op jit(solution)/shard_map/all_gather | solution.py:80
Sparse Core Ops, SparseCore 0:
  21.2 51.2 all-gather.5
  107.7 11.8 all-gather.3
where the time goes:
time: 136 us
  waiting for transfers between devices  54.8 us (40%)
  matrix products  51.5 us (38%)
  between operations  13.6 us (10%)
  other arithmetic  13.1 us (10%)
  local copies, waits for them, and re-layouts  2.79 us (2%)
    all_gather x1, waiting for transfers between devices, local(): lax.all_gather(block_state[None].astype(jnp.bfloat16), 'seq', axis=0, til...  42.7 us
    dot_general x1, matrix products, local(): jnp.einsum('iot,tiw->oiw', weight_tensors, value_matrix, preferred_elemen...  16 us
    dot_general x1, matrix products, local(): jnp.einsum('hfn,hfd->nhd', query_features(query_rows), earlier, precision...  12.1 us
    all_gather x1, waiting for transfers between devices, local(): lax.all_gather(normalized_rows, 'feat', axis=1, tiled=True)  12 us
    dot_general x1, matrix products, local(): jnp.dot(lax.all_gather(normalized_rows, 'feat', axis=1, tiled=True), w_ou...  9.36 us
    dot_general x1, matrix products, local(): jnp.dot(tokens, value_weight, preferred_element_type=jnp.float32)  4.81 us
    mul x1, other arithmetic, query_features(): jnp.einsum('nha,nhb->habn', as_float, as_float)  4.45 us
    convert_element_type x1, other arithmetic, local(): (numerator * scale).reshape(row_count, local_heads * DV)  4.11 us
  transfers between devices with their start and end apart: 2, of which 2 were waited for; matrix products, arithmetic and copies ran while one was open for 6% of the time, Pallas kernels for 0%

commit v1 on v0

--- a/solution.py
+++ b/solution.py
@@ -5,6 +5,27 @@
 
 DK = 16
 DV = 128
+
+
+def _detail_trails(block_in, chip_axis):
+    carry_in, extra, tmp = (lax.axis_size(chip_axis), lax.axis_index(chip_axis), block_in.shape[0])
+    rows = [(to_i, (to_i + 1) % carry_in) for to_i in range(carry_in)]
+    all_blocks = [(to_i, (to_i - 1) % carry_in) for to_i in range(carry_in)]
+    then = jnp.zeros((*block_in.shape[:0], carry_in * tmp, *block_in.shape[1:]), block_in.dtype)
+    then = lax.dynamic_update_slice_in_dim(then, block_in, extra * tmp, axis=0)
+    built = z_new = block_in
+    right_arr = carry_in // 2
+    k = 1
+    while k < right_arr + 1:
+        built = lax.ppermute(built, axis_name=chip_axis, perm=rows)
+        then = lax.dynamic_update_slice_in_dim(then, built, (extra - k) % carry_in * tmp, axis=0)
+        if k < carry_in - right_arr:
+            z_new = lax.ppermute(z_new, axis_name=chip_axis, perm=all_blocks)
+            then = lax.dynamic_update_slice_in_dim(
+                then, z_new, (extra + k) % carry_in * tmp, axis=0
+            )
+        k += 1
+    return then
 
 
 def key_features(key_rows):
@@ -52,9 +73,7 @@
     )
     zero_state = jnp.zeros(block_state.shape, jnp.float32)
     my_block = lax.axis_index("seq")
-    piece = lax.all_gather(
-        block_state[None].astype(jnp.bfloat16), "seq", axis=0, tiled=True
-    ).astype(jnp.float32)
+    piece = _detail_trails(block_state[None].astype(jnp.bfloat16), "seq").astype(jnp.float32)
     order = lax.broadcasted_iota(jnp.int32, (piece.shape[0],), 0)
     keep = (order < my_block).astype(jnp.float32)
     earlier = zero_state + jnp.sum(piece * keep[:, None, None, None], axis=0)

time: 136 us -> 115 us (0.85)
  waiting for transfers between devices: 54.8 us -> 25.6 us
  starting transfers between devices: 0.04 us -> 5.36 us
  local copies, waits for them, and re-layouts: 2.79 us -> 6.73 us
  other arithmetic: 13.1 us -> 11.5 us
    all_gather x1 -> x0, waiting for transfers between devices: 42.7 us -> none  [local(): lax.all_gather(block_state[None].astype(jnp.bfloat16), 'seq', axis=0, til...]
    ppermute x0 -> x3, waiting for transfers between devices: none -> 13.6 us  [the longest x2 13.6 us: _detail_trails(): built = lax.ppermute(built, axis_name=chip_axis, perm=rows)]
    ppermute x0 -> x3, starting transfers between devices: none -> 5.36 us  [the longest x2 3.34 us: _detail_trails(): built = lax.ppermute(built, axis_name=chip_axis, perm=rows)]
    dynamic_update_slice x0 -> x3, local copies, waits for them, and re-layouts: none -> 3.76 us  [the longest x2 2.52 us: _detail_trails(): lax.dynamic_update_slice_in_dim(then, built, (extra - k) % carry_in * tmp...]
    dot_general x1, matrix products: 1.7 us -> 4.85 us  [local(): jnp.einsum('hfn,nhd->hfd', key_features(key_rows), value_matrix, preferre...]
    reduce_sum x1, other arithmetic: 2.85 us -> 0.53 us  [local(): earlier = zero_state + jnp.sum(piece * keep[:, None, None, None], axis=0)]
    dot_general x1, matrix products: 3.7 us -> 1.51 us  [local(): jnp.dot(tokens, w_query, preferred_element_type=jnp.float32)]
    convert_element_type x1, other arithmetic: 4.11 us -> 1.96 us  [local(): (numerator * scale).reshape(row_count, local_heads * DV)]
  transfers between devices with their start and end apart: 2 -> 4, of which waited for: 2 -> 2; matrix products, arithmetic and copies ran while one was open for 6% -> 22% of each run, Pallas kernels for 0% -> 0%
where the time goes in v1:
time: 115 us; the launch traced here: 114 us
  matrix products  51.4 us (45%)
  waiting for transfers between devices  25.6 us (22%)
  between operations  13.6 us (12%)
  other arithmetic  11.5 us (10%)
  local copies, waits for them, and re-layouts  6.73 us (6%)
  starting transfers between devices  5.36 us (5%)
    dot_general x1, matrix products, local(): jnp.einsum('iot,tiw->oiw', weight_tensors, value_matrix, preferred_elemen...  15.3 us
    ppermute x2, waiting for transfers between devices, _detail_trails(): built = lax.ppermute(built, axis_name=chip_axis, perm=rows)  13.6 us
    all_gather x1, waiting for transfers between devices, local(): lax.all_gather(normalized_rows, 'feat', axis=1, tiled=True)  12 us
    dot_general x1, matrix products, local(): jnp.einsum('hfn,hfd->nhd', query_features(query_rows), earlier, precision...  10.7 us
    dot_general x1, matrix products, local(): jnp.dot(lax.all_gather(normalized_rows, 'feat', axis=1, tiled=True), w_ou...  9.36 us
    dot_general x1, matrix products, local(): jnp.dot(tokens, value_weight, preferred_element_type=jnp.float32)  5.78 us
    dot_general x1, matrix products, local(): jnp.einsum('hfn,nhd->hfd', key_features(key_rows), value_matrix, preferre...  4.85 us
    mul x1, other arithmetic, query_features(): jnp.einsum('nha,nhb->habn', as_float, as_float)  4.44 us
  transfers between devices with their start and end apart: 4, of which 2 were waited for; matrix products, arithmetic and copies ran while one was open for 22% of the time, Pallas kernels for 0%

profile of v1, /device:TPU:0, one launch (start us, length us, event | category | flops | bytes accessed | tf_op | source)
XLA Modules:
  0.0 114.3 jit_solution(14940290484713164260)
XLA Ops:
  6.5 0.0 copy-start
  6.5 0.0 all-gather.2.cloned.1.call-start
  6.5 1.0 copy-done
  7.6 0.0 copy-start.8
  7.6 3.9 %convolution_convert_fusion.3 = bf16[1024,128]{0,1:T(8,128)(2,1)S(1)} fusion(bf16[1024,2048]{1,0:T(8,128)(2,1)} %param.5, bf16[2048,128]{1,0:T(8,128)(2,1)S(1)} %copy-done), kind=kOutput, calls=%fused_computation.29 | convolution fusion | flops 537001984 | bytes 4980736 | tf_op jit(solution)/shard_map/dot_general | solution.py:62
  11.4 0.0 copy-start.6
  11.4 0.0 copy-start.1
  11.5 3.2 %multiply_convert_fusion = bf16[8,1024,16,16]{1,2,3,0:T(8,128)(2,1)} fusion(f32[8,1024,16]{1,2,0:T(8,128)S(1)} %convert_bitcast_fusion.1), kind=kLoop, calls=%fused_computation.9 | loop fusion | flops 4194304 | bytes 4718592 | tf_op jit(solution)/shard_map/convert.13
  14.7 0.0 copy-done.8
  14.7 0.0 copy-done.1
  14.7 5.8 %convolution_convert_fusion.1 = bf16[1024,1024]{0,1:T(8,128)(2,1)} fusion(bf16[1024,2048]{1,0:T(8,128)(2,1)S(1)} %copy-done.1, bf16[2048,1024]{1,0:T(8,128)(2,1)S(1)} %copy-done.8), kind=kOutput, calls=%fused_computation.25 | convolution fusion | flops 4296015872 | bytes 10485760 | tf_op jit(solution)/shard_map/dot_general | solution.py:67
  20.5 0.3 broadcast_in_dim.19
  20.8 0.0 copy-done.6
  20.8 0.0 copy-start.2
  20.8 0.0 copy-start.7
  20.8 4.8 %constant_dynamic-update-slice_fusion = (bf16[4,8,273,128]{3,2,1,0:T(8,128)(2,1)S(1)}, bf16[1,8,273,128]{3,2,1,0:T(8,128)(2,1)S(1)}) fusion(bf16[4,8,273,128]{3,2,1,0:T(8,128)(2,1)S(1)} %broadcast_in_dim.19, s32[]{:T(128)S(6)} %select_n.31, bf16[1024,8,128]{0,2,1:T(8,128)(2,1)} %bitcast.51, bf16[8,256,1024]{2,1,0:T(8,128)(2,1)} %bitcast.44, ...), kind=kOutput, calls=%fused_computation.39 | convolution fusion | flops 586220544 | bytes 7701508 | tf_op jit(solution)/shard_map/hfn,nhd->hfd/dot_general | solution.py:71
  25.7 0.9 copy.8
  26.6 3.1 %collective-permute-start = (bf16[1,8,273,128]{3,1,2,0:T(8,128)(2,1)}, bf16[1,8,273,128]{3,1,2,0:T(8,128)(2,1)}, u32[]{:S(2)}, u32[]{:S(2)}) collective-permute-start(bf16[1,8,273,128]{3,1,2,0:T(8,128)(2,1)} %copy.8), channel_id=1, source_target_pairs={{0,2},{2,4},{4,6},{6,0},{1,3},{3,5},{5,7},{7,1},{8,10},{10,12},{12... | collective-permute-start | bytes 1677320 | tf_op jit(solution)/shard_map/ppermute | solution.py:20
  29.6 2.0 %collective-permute-start.1 = (bf16[1,8,273,128]{3,1,2,0:T(8,128)(2,1)}, bf16[1,8,273,128]{3,1,2,0:T(8,128)(2,1)}, u32[]{:S(2)}, u32[]{:S(2)}) collective-permute-start(bf16[1,8,273,128]{3,1,2,0:T(8,128)(2,1)} %copy.8), channel_id=1, source_target_pairs={{0,6},{2,0},{4,2},{6,4},{1,7},{3,1},{5,3},{7,5},{8,14},{10,8},{12,... | collective-permute-start | bytes 1677320 | tf_op jit(solution)/shard_map/ppermute | solution.py:23
  31.7 1.3 %iota_compare_fusion = pred[1024,1024]{1,0:T(8,128)(4,1)} fusion(), kind=kLoop, calls=%fused_computation.21 | loop fusion | flops 1048576 | bytes 1048576 | tf_op jit(solution)/shard_map/ge | solution.py:83
  33.0 0.0 copy-done.2
  33.0 0.0 copy-done.7
  33.0 1.5 %convolution_convert_fusion.2 = bf16[1024,128]{0,1:T(8,128)(2,1)S(1)} fusion(bf16[1024,2048]{1,0:T(8,128)(2,1)S(1)} %copy-done.2, bf16[2048,128]{1,0:T(8,128)(2,1)S(1)} %copy-done.7), kind=kOutput, calls=%fused_computation.28 | convolution fusion | flops 537001984 | bytes 4980736 | tf_op jit(solution)/shard_map/dot_general | solution.py:57
  34.5 0.0 copy-start.4
  34.5 0.7 copy-done.4
  35.2 15.3 %fusion = f32[8,128,1024]{2,1,0:T(8,128)} fusion(bf16[1024,8,128]{0,2,1:T(8,128)(2,1)} %bitcast.52, pred[1024,1024]{1,0:T(8,128)(4,1)} %iota_compare_fusion, bf16[1024,8,16]{0,2,1:T(8,128)(2,1)} %bitcast.46, bf16[1024,8,16]{0,2,1:T(8,128)(2,1)} %bitcast.50), kind=kOutput, calls=%fused_computation.1 | convolution fusion | flops 2474639360 | bytes 7864320 | tf_op jit(solution)/shard_map/iot,tiw->oiw/dot_general | solution.py:89
  50.6 0.0 copy-start.5
  50.6 4.4 %multiply_multiply_fusion = f32[8,1024,16,16]{1,2,3,0:T(8,128)} fusion(f32[8,1024,16]{1,2,0:T(8,128)S(1)} %convert_bitcast_fusion), kind=kLoop, calls=%fused_computation.8 | loop fusion | flops 4194304 | bytes 8912896 | tf_op jit(solution)/shard_map/mul | solution.py:46
  55.0 0.0 copy-done.5
  55.1 0.0 collective-permute-done
  55.1 0.3 collective-permute-start.2
  55.4 0.0 copy-start.3
  55.4 1.3 %copy_dynamic-update-slice_fusion.2 = bf16[4,8,273,128]{3,2,1,0:T(8,128)(2,1)S(1)} fusion(bf16[4,8,273,128]{3,2,1,0:T(8,128)(2,1)S(1)} %get-tuple-element.5, s32[]{:T(128)S(6)} %select_n.33, bf16[1,8,273,128]{3,1,2,0:T(8,128)(2,1)} %collective-permute-done), kind=kLoop, calls=%fused_computation.34 | loop fusion | bytes 1132548 | tf_op jit(solution)/shard_map/dynamic_update_slice | solution.py:21
  56.8 0.0 collective-permute-done.1
  56.8 1.2 %copy_dynamic-update-slice_fusion.1 = bf16[4,8,273,128]{3,2,1,0:T(8,128)(2,1)S(1)} fusion(bf16[4,8,273,128]{3,2,1,0:T(8,128)(2,1)S(1)} %copy_dynamic-update-slice_fusion.2, s32[]{:T(128)S(6)} %select_n.35, bf16[1,8,273,128]{3,1,2,0:T(8,128)(2,1)} %collective-permute-done.1), kind=kLoop, calls=%fused_computation.33 | loop fusion | bytes 1132548 | tf_op jit(solution)/shard_map/dynamic_update_slice | solution.py:24
  58.0 13.6 %collective-permute-done.2 = bf16[1,8,273,128]{3,1,2,0:T(8,128)(2,1)} collective-permute-done((bf16[1,8,273,128]{3,1,2,0:T(8,128)(2,1)}, bf16[1,8,273,128]{3,1,2,0:T(8,128)(2,1)}, u32[]{:S(2)}, u32[]{:S(2)}) %collective-permute-start.2) | collective-permute-done | bytes 559136 | tf_op jit(solution)/shard_map/ppermute | solution.py:20
  71.6 1.2 %copy_dynamic-update-slice_fusion = bf16[4,8,273,128]{3,2,1,0:T(8,128)(2,1)S(1)} fusion(bf16[4,8,273,128]{3,2,1,0:T(8,128)(2,1)S(1)} %copy_dynamic-update-slice_fusion.1, s32[]{:T(128)S(6)} %select_n.37, bf16[1,8,273,128]{3,1,2,0:T(8,128)(2,1)} %collective-permute-done.2), kind=kLoop, calls=%fused_computation.32 | loop fusion | bytes 1132548 | tf_op jit(solution)/shard_map/dynamic_update_slice | solution.py:21
  72.8 0.5 multiply_reduce_fusion
  73.3 0.0 copy-done.3
  73.3 10.7 %fusion.13 = (f32[1024,8]{0,1:T(8,128)S(1)}, f32[8,128,1024]{2,1,0:T(8,128)S(1)}) fusion(f32[8,128,1024]{2,1,0:T(8,128)S(1)} %copy-done.3, f32[8,273,128]{2,1,0:T(8,128)S(1)} %multiply_reduce_fusion, f32[8,256,1024]{2,1,0:T(8,128)} %bitcast.42, f32[8,16,1024]{2,1,0:T(8,128)S(1)} %fusion.25, f32[273]{0:T(512)S(1)} %pad.clone), kind=kOutput, calls=%fused_computation.19 | convolution fusion | flops 3442745344 | bytes 18453572 | tf_op jit(solution)/shard_map/hfn,hfd->nhd/dot_general | solution.py:92
  84.1 2.0 %fusion.14 = bf16[1024,8,128]{0,2,1:T(8,128)(2,1)} fusion(f32[8,128,1024]{2,1,0:T(8,128)S(1)} %get-tuple-element.8, f32[1024,8]{0,1:T(8,128)S(1)} %add_rsqrt_fusion), kind=kLoop, calls=%fused_computation.20 | loop fusion | flops 2097152 | bytes 6324224 | tf_op jit(solution)/shard_map/convert_element_type | solution.py:97
  86.0 0.0 all-gather.2.cloned.1.call-update
  86.1 12.0 %all-gather.2.cloned.1.call-done = bf16[1024,2048]{0,1:T(8,128)(2,1)} async-done(((bf16[1024,1024]{0,1:T(8,128)(2,1)}), bf16[1024,2048]{0,1:T(8,128)(2,1)}) %all-gather.2.cloned.1.call-update) | async-done | bytes 4194320 | tf_op jit(solution)/shard_map/all_gather | solution.py:99
  98.1 9.4 %convolution_convert_fusion = bf16[1024,1024]{1,0:T(8,128)(2,1)} fusion(bf16[1024,2048]{0,1:T(8,128)(2,1)} %all-gather.2.cloned.1.call-done, bf16[2048,1024]{1,0:T(8,128)(2,1)} %param.9), kind=kOutput, calls=%fused_computation.24 | convolution fusion | flops 4296015872 | bytes 10485760 | tf_op jit(solution)/shard_map/dot_general | solution.py:98
  (7 shorter events, 0.2 us)
Async XLA Ops:
  6.5 1.0 copy-start
  6.5 91.5 %all-gather.2.cloned.1.call-start = ((), (), s32[]{:S(2)}) async-start(), calls=%async_computation | async-start | bytes 6291456 | tf_op jit(solution)/shard_map/all_gather | solution.py:99
  7.6 7.1 %copy-start.8 = (bf16[2048,1024]{1,0:T(8,128)(2,1)S(1)}, bf16[2048,1024]{1,0:T(8,128)(2,1)}, u32[]{:S(2)}) copy-start(bf16[2048,1024]{1,0:T(8,128)(2,1)} %param.8) | copy-start | bytes 12582916
  11.4 9.4 %copy-start.6 = (bf16[1024,128]{0,1:T(8,128)(2,1)}, bf16[1024,128]{0,1:T(8,128)(2,1)S(1)}, u32[]{:S(2)}) copy-start(bf16[1024,128]{0,1:T(8,128)(2,1)S(1)} %convolution_convert_fusion.3) | copy-start | bytes 786436
  11.4 3.3 %copy-start.1 = (bf16[1024,2048]{1,0:T(8,128)(2,1)S(1)}, bf16[1024,2048]{1,0:T(8,128)(2,1)}, u32[]{:S(2)}) copy-start(bf16[1024,2048]{1,0:T(8,128)(2,1)} %param.5) | copy-start | bytes 12582916
  20.8 12.1 %copy-start.2 = (bf16[1024,2048]{1,0:T(8,128)(2,1)S(1)}, bf16[1024,2048]{1,0:T(8,128)(2,1)}, u32[]{:S(2)}) copy-start(bf16[1024,2048]{1,0:T(8,128)(2,1)} %param.5) | copy-start | bytes 12582916
  20.8 12.1 %copy-start.7 = (bf16[2048,128]{1,0:T(8,128)(2,1)S(1)}, bf16[2048,128]{1,0:T(8,128)(2,1)}, u32[]{:S(2)}) copy-start(bf16[2048,128]{1,0:T(8,128)(2,1)} %param.6) | copy-start | bytes 1572868
  26.6 28.5 %collective-permute-start = (bf16[1,8,273,128]{3,1,2,0:T(8,128)(2,1)}, bf16[1,8,273,128]{3,1,2,0:T(8,128)(2,1)}, u32[]{:S(2)}, u32[]{:S(2)}) collective-permute-start(bf16[1,8,273,128]{3,1,2,0:T(8,128)(2,1)} %copy.8), channel_id=1, source_target_pairs={{0,2},{2,4},{4,6},{6,0},{1,3},{3,5},{5,7},{7,1},{8,10},{10,12},{12... | collective-permute-start | bytes 1677320 | tf_op jit(solution)/shard_map/ppermute | solution.py:20
  29.6 27.1 %collective-permute-start.1 = (bf16[1,8,273,128]{3,1,2,0:T(8,128)(2,1)}, bf16[1,8,273,128]{3,1,2,0:T(8,128)(2,1)}, u32[]{:S(2)}, u32[]{:S(2)}) collective-permute-start(bf16[1,8,273,128]{3,1,2,0:T(8,128)(2,1)} %copy.8), channel_id=1, source_target_pairs={{0,6},{2,0},{4,2},{6,4},{1,7},{3,1},{5,3},{7,5},{8,14},{10,8},{12,... | collective-permute-start | bytes 1677320 | tf_op jit(solution)/shard_map/ppermute | solution.py:23
  34.5 0.7 copy-start.4
  50.6 4.4 %copy-start.5 = (bf16[1024,128]{0,1:T(8,128)(2,1)S(1)}, bf16[1024,128]{0,1:T(8,128)(2,1)}, u32[]{:S(2)}) copy-start(bf16[1024,128]{0,1:T(8,128)(2,1)} %copy-done.4) | copy-start | bytes 786436
  55.1 16.5 %collective-permute-start.2 = (bf16[1,8,273,128]{3,1,2,0:T(8,128)(2,1)}, bf16[1,8,273,128]{3,1,2,0:T(8,128)(2,1)}, u32[]{:S(2)}, u32[]{:S(2)}) collective-permute-start(bf16[1,8,273,128]{3,1,2,0:T(8,128)(2,1)} %collective-permute-done), channel_id=1, source_target_pairs={{0,2},{2,4},{4,6},{6,0},{1,3},{3,5},{5,7},{7,1},{8,10},{10,12},{12... | collective-permute-start | bytes 1677320 | tf_op jit(solution)/shard_map/ppermute | solution.py:20
  55.4 17.9 %copy-start.3 = (f32[8,128,1024]{2,1,0:T(8,128)S(1)}, f32[8,128,1024]{2,1,0:T(8,128)}, u32[]{:S(2)}) copy-start(f32[8,128,1024]{2,1,0:T(8,128)} %fusion) | copy-start | bytes 12582916
Sparse Core Ops, SparseCore 0:
  86.2 11.8 all-gather.1
